TPU v7x, 256 devices: a whole 4x4x8 slice. The times are simulated.
256 devices in a mesh: ex: 2 (over core), slab: 128 (over z, y, x).
Axes of the slice: x: 4, y: 4, z: 8, core: 2. Of those that a mesh axis runs over, the one named last changes fastest.
Arguments:
- volume: bfloat16 [2, 16, 128, 32, 128], P('ex', None, 'slab'), may hold values from -6 to 6
- cotangent: bfloat16 [2, 16, 128, 32, 128], P('ex', None, 'slab')
- gate_mask: int32 [2, 2, 128, 32, 128], P('ex', None, 'slab'), may hold values 0 or 1
- loss_scale: float32 [2], P('ex'), may hold values from 0.05 to 5
- canary: int32 [2], P('ex'), may hold values from 0 to 15
- kernels: bfloat16 [2, 32, 432], replicated, may hold values from -0.3125 to 0.3125
Outputs:
- input_grad: float32 [2, 16, 128, 32, 128], P('ex', None, 'slab')
- kernel_grad: float32 [2, 32, 432], replicated
All inputs are finite; a program needn't handle non-finite values. No bound on the sum of `gate_mask` on one device may be relied on, other than what follows from the above.
Results may differ from a plain program's by a relative error of at most 0.0037.
Values may be sent and summed in bfloat16 or wider, within the bound.
A program may use at most 64 MiB of HBM per device.

v0:
```python
import jax
import jax.numpy as jnp
from jax import lax
from jax.sharding import PartitionSpec as P


def with_halo(array, sides, width):
    for axis, dim in sides:
        peers, length = (lax.axis_size(axis), array.shape[dim])
        up = [(i, (i + 1) % peers) for i in range(peers - 1)]
        down = [(j, i) for i, j in up]
        last = lax.slice_in_dim(array, length - width, length, axis=dim)
        leading = lax.slice_in_dim(array, 0, width, axis=dim)
        before = lax.ppermute(last, axis, up)
        after = lax.ppermute(leading, axis, down)
        array = jnp.concatenate([before, array, after], axis=dim)
    return array


def columns(extended):
    zs = extended.shape[2] - 2
    hs, ws = (extended.shape[3], extended.shape[4])
    padded = jnp.pad(extended, ((0, 0), (0, 0), (0, 0), (1, 1), (1, 1)))
    taps = []
    for dz in range(3):
        for dh in range(3):
            for dw in range(3):
                taps.append(padded[:, :, dz : dz + zs, dh : dh + hs, dw : dw + ws])
    stacked = jnp.stack(taps, axis=1)
    return stacked.reshape((extended.shape[0], 27 * extended.shape[1], zs, hs, ws))


def back_columns(extended):
    zs = extended.shape[2] - 2
    hs, ws = (extended.shape[3], extended.shape[4])
    padded = jnp.pad(extended, ((0, 0), (0, 0), (0, 0), (1, 1), (1, 1)))
    taps = []
    for dz in range(3):
        for dh in range(3):
            for dw in range(3):
                taps.append(
                    padded[:, :, 2 - dz : 2 - dz + zs, 2 - dh : 2 - dh + hs, 2 - dw : 2 - dw + ws]
                )
    return jnp.stack(taps, axis=1)


def layer_forward(field, kernel):
    extended = with_halo(field, (("slab", 2),), 1)
    patches = columns(extended)
    pre = jnp.einsum("ok,ekzhw->eozhw", kernel, patches, preferred_element_type=jnp.float32)
    return (pre, patches)


def layer_backward(delta, kernel, patches):
    grads = jnp.einsum("eozhw,ekzhw->eok", delta, patches, preferred_element_type=jnp.float32)
    extended = with_halo(delta, (("slab", 2),), 1)
    width = kernel.shape[1] // 27
    shaped = kernel.reshape((kernel.shape[0], 27, width))
    spread = jnp.einsum(
        "otc,etozhw->eczhw", shaped, back_columns(extended), preferred_element_type=jnp.float32
    )
    return (grads, spread)


def per_device(volume, cotangent, gate_mask, loss_scale, canary, kernels):
    chans = volume.shape[1]
    local_ex = volume.shape[0]
    mask_one = gate_mask[:, 0][:, None].astype(jnp.float32)
    mask_two = gate_mask[:, 1][:, None].astype(jnp.float32)
    pre_one, patches_one = layer_forward(volume, kernels[0])
    value_one = pre_one[:, :chans]
    sig_one = jax.nn.sigmoid(pre_one[:, chans:])
    hidden = (volume.astype(jnp.float32) + value_one * sig_one * mask_one).astype(jnp.bfloat16)
    pre_two, patches_two = layer_forward(hidden, kernels[1])
    value_two = pre_two[:, :chans]
    sig_two = jax.nn.sigmoid(pre_two[:, chans:])
    channel_ids = jnp.arange(chans, dtype=jnp.int32)
    weights = 1.0 + 2.0 * (channel_ids[None, :] == canary[:, None]).astype(jnp.float32)
    weights = weights * loss_scale[:, None]
    grad_out = cotangent.astype(jnp.float32) * weights[:, :, None, None, None]
    delta_two = jnp.concatenate(
        [
            grad_out * sig_two * mask_two,
            grad_out * value_two * sig_two * (1.0 - sig_two) * mask_two,
        ],
        axis=1,
    ).astype(jnp.bfloat16)
    grad_two, spread_two = layer_backward(delta_two, kernels[1], patches_two)
    grad_hidden = grad_out + spread_two
    delta_one = jnp.concatenate(
        [
            grad_hidden * sig_one * mask_one,
            grad_hidden * value_one * sig_one * (1.0 - sig_one) * mask_one,
        ],
        axis=1,
    ).astype(jnp.bfloat16)
    grad_one, spread_one = layer_backward(delta_one, kernels[0], patches_one)
    input_grad = grad_hidden + spread_one
    stacked = jnp.stack([grad_one, grad_two], axis=1)
    flat = stacked.reshape((local_ex, -1))
    depth = volume.shape[2] * lax.axis_size("slab")
    bound = 20.0 * jnp.sqrt(jnp.float32(depth * volume.shape[3] * volume.shape[4]))
    examples = local_ex * lax.axis_size("ex")
    scaling = jnp.sqrt(jnp.float32(108 * chans * chans)) / (bound * jnp.sqrt(jnp.float32(examples)))
    summed = lax.psum(flat, "slab")
    norm = jnp.sqrt(jnp.sum(summed * summed, axis=1) + 1e-06)
    factor = jnp.minimum(1.0, bound / norm)
    local_total = jnp.sum(summed * factor[:, None], axis=0)
    total = lax.psum(local_total, "ex")
    kernel_grad = (total * scaling).reshape(kernels.shape)
    return (input_grad, kernel_grad)


def solution(mesh):
    placed = (
        P("ex", None, "slab", None, None),
        P("ex", None, "slab", None, None),
        P("ex", None, "slab", None, None),
        P("ex"),
        P("ex"),
        P(),
    )
    return jax.shard_map(
        per_device,
        mesh=mesh,
        in_specs=placed,
        out_specs=(P("ex", None, "slab", None, None), P()),
        check_vma=False,
    )
```

profile of v0, /device:TPU:1, one launch (start us, length us, event | category | flops | bytes accessed | tf_op | source)
XLA Modules:
  0.0 345.2 jit_solution(6189408591076951782)
XLA Ops:
  7.2 1.3 collective-permute-start.1
  8.5 4.6 %collective-permute-start = (bf16[1,16,1,32,128]{4,3,1,2,0:T(8,128)(2,1)}, bf16[1,16,1,32,128]{4,3,1,2,0:T(8,128)(2,1)S(1)}, u32[]{:S(2)}, u32[]{:S(2)}) collective-permute-start(bf16[1,16,1,32,128]{4,3,1,2,0:T(8,128)(2,1)} %bitcast.510), channel_id=1, source_target_pairs={{0,1},{1,2},{2,3},{3,4},{4,5},{5,6},{6,7},{7,8},{8,9},{9,10},{10,1... | collective-permute-start | bytes 393224 | tf_op jit(solution)/shard_map/ppermute | solution.py:14
  13.1 1.3 convert_bitcast_fusion
  14.4 0.9 collective-permute-done
  15.3 1.6 select_maximum_fusion.5
  19.8 1.4 copy.24
  21.2 0.7 convolution_bitcast_fusion
  22.0 0.8 copy-done.4
  22.8 0.8 add_convert_fusion
  23.5 1.3 collective-permute-start.3
  24.8 5.0 %collective-permute-start.2 = (bf16[1,16,1,32,128]{4,1,3,2,0:T(8,128)(2,1)}, bf16[1,16,1,32,128]{4,1,3,2,0:T(8,128)(2,1)}, u32[]{:S(2)}, u32[]{:S(2)}) collective-permute-start(bf16[1,16,1,32,128]{4,1,3,2,0:T(8,128)(2,1)} %add_convert_fusion), channel_id=1, source_target_pairs={{0,1},{1,2},{2,3},{3,4},{4,5},{5,6},{6,7},{7,8},{8,9},{9,10},{10,1... | collective-permute-start | bytes 393224 | tf_op jit(solution)/shard_map/ppermute | solution.py:14
  29.8 0.6 fusion.118
  31.7 1.5 copy.27
  33.2 1.4 select_maximum_fusion.7
  35.0 0.9 constant_dynamic-update-slice_fusion.49
  36.7 0.9 constant_dynamic-update-slice_fusion.40
  38.4 0.9 constant_dynamic-update-slice_fusion.31
  39.7 0.9 copy.25
  40.7 1.2 fusion.22
  41.9 0.2 multiply_convert_fusion.2
  42.1 1.3 collective-permute-start.5
  43.4 4.2 %collective-permute-start.4 = (bf16[1,32,1,32,128]{4,1,3,2,0:T(8,128)(2,1)S(1)}, bf16[1,32,1,32,128]{4,1,3,2,0:T(8,128)(2,1)S(1)}, u32[]{:S(2)}, u32[]{:S(2)}) collective-permute-start(bf16[1,32,1,32,128]{4,1,3,2,0:T(8,128)(2,1)S(1)} %pad_maximum_fusion), channel_id=1, source_target_pairs={{0,1},{1,2},{2,3},{3,4},{4,5},{5,6},{6,7},{7,8},{8,9},{9,10},{10,1... | collective-permute-start | bytes 786440 | tf_op jit(solution)/shard_map/ppermute | solution.py:14
  47.6 1.2 fusion.37
  48.9 0.4 collective-permute-done.5
  49.3 1.5 collective-permute-done.4
  50.7 2.3 select_maximum_fusion.3
  53.2 0.2 fusion.92
  53.4 0.2 fusion.90
  53.7 0.2 fusion.88
  53.9 0.2 fusion.87
  54.2 0.2 fusion.85
  54.4 0.2 fusion.84
  56.6 1.9 multiply_convert_fusion.1
  58.5 1.1 convolution_bitcast_fusion.1
  59.7 0.9 reshape.189
  60.6 0.9 copy.29
  61.5 230.7 %all-reduce.7.cloned.1.call-done = f32[1,27648]{1,0:T(1,128)} async-done(((f32[1,27648]{1,0:T(1,128)}), f32[1,27648]{1,0:T(1,128)}) %all-reduce.7.cloned.1.call-update) | async-done | bytes 110608 | tf_op jit(solution)/shard_map/psum | solution.py:105
  292.2 1.7 multiply_reduce_fusion
  294.7 1.6 broadcast_multiply_fusion.1
  296.3 1.0 pad_maximum_fusion.1
  297.3 1.3 collective-permute-start.7
  298.6 4.2 %collective-permute-start.6 = (bf16[1,32,1,32,128]{4,1,3,2,0:T(8,128)(2,1)S(1)}, bf16[1,32,1,32,128]{4,1,3,2,0:T(8,128)(2,1)S(1)}, u32[]{:S(2)}, u32[]{:S(2)}) collective-permute-start(bf16[1,32,1,32,128]{4,1,3,2,0:T(8,128)(2,1)S(1)} %pad_maximum_fusion.1), channel_id=1, source_target_pairs={{0,1},{1,2},{2,3},{3,4},{4,5},{5,6},{6,7},{7,8},{8,9},{9,10},{10,1... | collective-permute-start | bytes 786440 | tf_op jit(solution)/shard_map/ppermute | solution.py:14
  302.8 25.1 %all-reduce.9.cloned.1.call-done = f32[27648]{0:T(1024)} async-done(((f32[27648]{0:T(1024)}), f32[27648]{0:T(1024)}) %all-reduce.9.cloned.1.call-update) | async-done | bytes 110608 | tf_op jit(solution)/shard_map/psum | solution.py:109
  327.9 0.9 broadcast_multiply_fusion
  328.8 0.8 reshape.190
  329.6 3.2 select_maximum_fusion
  336.3 1.2 fusion.31
  337.6 0.8 copy.32
  (138 shorter events, 10.8 us)
Async XLA Ops:
  7.2 11.1 %copy-start.6 = (bf16[1,16,1,32,128]{4,3,2,1,0:T(8,128)(2,1)S(1)}, bf16[1,16,1,32,128]{4,3,2,1,0:T(8,128)(2,1)}, u32[]{:S(2)}) copy-start(bf16[1,16,1,32,128]{4,3,2,1,0:T(8,128)(2,1)} %param.6) | copy-start | bytes 393220
  7.2 285.1 %all-reduce.7.cloned.1.call-start = ((), (), s32[]{:S(2)}) async-start(), calls=%async_computation | async-start | bytes 221184 | tf_op jit(solution)/shard_map/psum | solution.py:105
  7.2 8.1 %collective-permute-start.1 = (bf16[1,16,1,32,128]{4,3,2,1,0:T(8,128)(2,1)}, bf16[1,16,1,32,128]{4,3,2,1,0:T(8,128)(2,1)S(1)}, u32[]{:S(2)}, u32[]{:S(2)}) collective-permute-start(bf16[1,16,1,32,128]{4,3,2,1,0:T(8,128)(2,1)} %param.6), channel_id=1, source_target_pairs={{1,0},{2,1},{3,2},{4,3},{5,4},{6,5},{7,6},{8,7},{9,8},{10,9},{11,1... | collective-permute-start | bytes 393224 | tf_op jit(solution)/shard_map/ppermute | solution.py:15
  8.5 6.8 %collective-permute-start = (bf16[1,16,1,32,128]{4,3,1,2,0:T(8,128)(2,1)}, bf16[1,16,1,32,128]{4,3,1,2,0:T(8,128)(2,1)S(1)}, u32[]{:S(2)}, u32[]{:S(2)}) collective-permute-start(bf16[1,16,1,32,128]{4,3,1,2,0:T(8,128)(2,1)} %bitcast.510), channel_id=1, source_target_pairs={{0,1},{1,2},{2,3},{3,4},{4,5},{5,6},{6,7},{7,8},{8,9},{9,10},{10,1... | collective-permute-start | bytes 393224 | tf_op jit(solution)/shard_map/ppermute | solution.py:14
  19.8 1.4 copy-start.11
  21.2 1.6 copy-start.7
  22.0 0.8 copy-start.4
  23.5 9.7 %collective-permute-start.3 = (bf16[1,16,1,32,128]{4,1,3,2,0:T(8,128)(2,1)}, bf16[1,16,1,32,128]{4,1,3,2,0:T(8,128)(2,1)}, u32[]{:S(2)}, u32[]{:S(2)}) collective-permute-start(bf16[1,16,1,32,128]{4,1,3,2,0:T(8,128)(2,1)} %add_convert_fusion), channel_id=1, source_target_pairs={{1,0},{2,1},{3,2},{4,3},{5,4},{6,5},{7,6},{8,7},{9,8},{10,9},{11,1... | collective-permute-start | bytes 393224 | tf_op jit(solution)/shard_map/ppermute | solution.py:15
  24.8 8.4 %collective-permute-start.2 = (bf16[1,16,1,32,128]{4,1,3,2,0:T(8,128)(2,1)}, bf16[1,16,1,32,128]{4,1,3,2,0:T(8,128)(2,1)}, u32[]{:S(2)}, u32[]{:S(2)}) collective-permute-start(bf16[1,16,1,32,128]{4,1,3,2,0:T(8,128)(2,1)} %add_convert_fusion), channel_id=1, source_target_pairs={{0,1},{1,2},{2,3},{3,4},{4,5},{5,6},{6,7},{7,8},{8,9},{9,10},{10,1... | collective-permute-start | bytes 393224 | tf_op jit(solution)/shard_map/ppermute | solution.py:14
  39.7 1.0 copy-start.12
  40.7 1.2 copy-start.9
  40.7 1.2 copy-start.13
  42.1 7.1 %collective-permute-start.5 = (bf16[1,32,1,32,128]{4,1,3,2,0:T(8,128)(2,1)S(1)}, bf16[1,32,1,32,128]{4,1,3,2,0:T(8,128)(2,1)S(1)}, u32[]{:S(2)}, u32[]{:S(2)}) collective-permute-start(bf16[1,32,1,32,128]{4,1,3,2,0:T(8,128)(2,1)S(1)} %pad_maximum_fusion), channel_id=1, source_target_pairs={{1,0},{2,1},{3,2},{4,3},{5,4},{6,5},{7,6},{8,7},{9,8},{10,9},{11,1... | collective-permute-start | bytes 786440 | tf_op jit(solution)/shard_map/ppermute | solution.py:15
  43.4 7.3 %collective-permute-start.4 = (bf16[1,32,1,32,128]{4,1,3,2,0:T(8,128)(2,1)S(1)}, bf16[1,32,1,32,128]{4,1,3,2,0:T(8,128)(2,1)S(1)}, u32[]{:S(2)}, u32[]{:S(2)}) collective-permute-start(bf16[1,32,1,32,128]{4,1,3,2,0:T(8,128)(2,1)S(1)} %pad_maximum_fusion), channel_id=1, source_target_pairs={{0,1},{1,2},{2,3},{3,4},{4,5},{5,6},{6,7},{7,8},{8,9},{9,10},{10,1... | collective-permute-start | bytes 786440 | tf_op jit(solution)/shard_map/ppermute | solution.py:14
  54.9 1.7 copy-start.5
  54.9 1.7 copy-start.10
  58.5 1.1 copy-start
  58.5 1.1 copy-start.2
  60.6 267.4 %all-reduce.9.cloned.1.call-start = ((), (), s32[]{:S(2)}) async-start(), calls=%async_computation.1 | async-start | bytes 221184 | tf_op jit(solution)/shard_map/psum | solution.py:109
  297.3 32.3 %collective-permute-start.7 = (bf16[1,32,1,32,128]{4,1,3,2,0:T(8,128)(2,1)S(1)}, bf16[1,32,1,32,128]{4,1,3,2,0:T(8,128)(2,1)S(1)}, u32[]{:S(2)}, u32[]{:S(2)}) collective-permute-start(bf16[1,32,1,32,128]{4,1,3,2,0:T(8,128)(2,1)S(1)} %pad_maximum_fusion.1), channel_id=1, source_target_pairs={{1,0},{2,1},{3,2},{4,3},{5,4},{6,5},{7,6},{8,7},{9,8},{10,9},{11,1... | collective-permute-start | bytes 786440 | tf_op jit(solution)/shard_map/ppermute | solution.py:15
  298.6 31.1 %collective-permute-start.6 = (bf16[1,32,1,32,128]{4,1,3,2,0:T(8,128)(2,1)S(1)}, bf16[1,32,1,32,128]{4,1,3,2,0:T(8,128)(2,1)S(1)}, u32[]{:S(2)}, u32[]{:S(2)}) collective-permute-start(bf16[1,32,1,32,128]{4,1,3,2,0:T(8,128)(2,1)S(1)} %pad_maximum_fusion.1), channel_id=1, source_target_pairs={{0,1},{1,2},{2,3},{3,4},{4,5},{5,6},{6,7},{7,8},{8,9},{9,10},{10,1... | collective-permute-start | bytes 786440 | tf_op jit(solution)/shard_map/ppermute | solution.py:14
  332.8 1.8 copy-start.1
  332.8 1.8 copy-start.3
  334.6 1.7 copy-start.8
Sparse Core Ops, SparseCore 0:
  60.7 231.5 all-reduce.6
  296.4 31.4 all-reduce.8
where the time goes:
time: 346 us; the launch traced here: 345 us
  waiting for transfers between devices  259 us (75%)
  starting transfers between devices  23.2 us (7%)
  local copies, waits for them, and re-layouts  22.9 us (7%)
  between operations  16.9 us (5%)
  other arithmetic  16.1 us (5%)
  matrix products  7.43 us (2%)
    psum x1, waiting for transfers between devices, per_device(): summed = lax.psum(flat, 'slab')  231 us
    psum x1, waiting for transfers between devices, per_device(): total = lax.psum(local_total, 'ex')  25.1 us
    ppermute x4, starting transfers between devices, with_halo(): before = lax.ppermute(last, axis, up)  17.9 us
    unnamed x131, local copies, waits for them, and re-layouts  15.5 us
    concatenate x4, other arithmetic, with_halo(): array = jnp.concatenate([before, array, after], axis=dim)  8.49 us
  transfers between devices with their start and end apart: 10, of which 5 were waited for; matrix products, arithmetic and copies ran while one was open for 2% of the time, Pallas kernels for 0%

commit v1 on v0

--- a/solution.py
+++ b/solution.py
@@ -102,7 +102,8 @@
     bound = 20.0 * jnp.sqrt(jnp.float32(depth * volume.shape[3] * volume.shape[4]))
     examples = local_ex * lax.axis_size("ex")
     scaling = jnp.sqrt(jnp.float32(108 * chans * chans)) / (bound * jnp.sqrt(jnp.float32(examples)))
-    summed = lax.psum(flat, "slab")
+    parts = lax.all_gather(flat, "slab")
+    summed = jnp.sum(parts, axis=0)
     norm = jnp.sqrt(jnp.sum(summed * summed, axis=1) + 1e-06)
     factor = jnp.minimum(1.0, bound / norm)
     local_total = jnp.sum(summed * factor[:, None], axis=0)

time: 346 us -> 272 us (0.79)
  waiting for transfers between devices: 259 us -> 154 us
  local copies, waits for them, and re-layouts: 22.9 us -> 40.4 us
  other arithmetic: 16.1 us -> 25.4 us
    psum x1 -> x0, waiting for transfers between devices: 231 us -> none  [per_device(): summed = lax.psum(flat, 'slab')]
    all_gather x0 -> x1, waiting for transfers between devices: none -> 127 us  [per_device(): parts = lax.all_gather(flat, 'slab')]
    unnamed x131, local copies, waits for them, and re-layouts: 15.5 us -> 32.3 us
    reduce_sum x0 -> x1, other arithmetic: none -> 10.7 us  [per_device(): summed = jnp.sum(parts, axis=0)]
  transfers between devices with their start and end apart: 10 -> 10, of which waited for: 5 -> 7; matrix products, arithmetic and copies ran while one was open for 2% -> 13% of each run, Pallas kernels for 0% -> 0%
where the time goes in v1:
time: 272 us; the launch traced here: 271 us
  waiting for transfers between devices  154 us (57%)
  local copies, waits for them, and re-layouts  40.4 us (15%)
  other arithmetic  25.4 us (9%)
  starting transfers between devices  23.9 us (9%)
  between operations  16.7 us (6%)
  matrix products  10.4 us (4%)
    all_gather x1, waiting for transfers between devices, per_device(): parts = lax.all_gather(flat, 'slab')  127 us
    unnamed x131, local copies, waits for them, and re-layouts  32.3 us
    psum x1, waiting for transfers between devices, per_device(): total = lax.psum(local_total, 'ex')  22.3 us
    ppermute x4, starting transfers between devices, with_halo(): before = lax.ppermute(last, axis, up)  18.7 us
    reduce_sum x1, other arithmetic, per_device(): summed = jnp.sum(parts, axis=0)  10.7 us
    concatenate x4, other arithmetic, with_halo(): array = jnp.concatenate([before, array, after], axis=dim)  8.48 us
    dot_general x2, matrix products, layer_backward(): jnp.einsum('otc,etozhw->eczhw', shaped, back_columns(extended), preferred...  6.18 us
  transfers between devices with their start and end apart: 10, of which 7 were waited for; matrix products, arithmetic and copies ran while one was open for 13% of the time, Pallas kernels for 0%

profile of v1, /device:TPU:1, one launch (start us, length us, event | category | flops | bytes accessed | tf_op | source)
XLA Modules:
  0.0 271.3 jit_solution(11392163191259742988)
XLA Ops:
  7.2 1.3 collective-permute-start.1
  8.5 4.6 %collective-permute-start = (bf16[1,16,1,32,128]{4,3,1,2,0:T(8,128)(2,1)}, bf16[1,16,1,32,128]{4,3,1,2,0:T(8,128)(2,1)S(1)}, u32[]{:S(2)}, u32[]{:S(2)}) collective-permute-start(bf16[1,16,1,32,128]{4,3,1,2,0:T(8,128)(2,1)} %bitcast.509), channel_id=1, source_target_pairs={{0,1},{1,2},{2,3},{3,4},{4,5},{5,6},{6,7},{7,8},{8,9},{9,10},{10,1... | collective-permute-start | bytes 393224 | tf_op jit(solution)/shard_map/ppermute | solution.py:14
  13.1 1.3 convert_bitcast_fusion
  14.4 0.9 collective-permute-done
  15.3 1.6 select_maximum_fusion.5
  19.8 1.4 copy.38
  23.5 1.3 collective-permute-start.3
  24.8 5.0 %collective-permute-start.2 = (bf16[1,16,1,32,128]{4,1,3,2,0:T(8,128)(2,1)}, bf16[1,16,1,32,128]{4,1,3,2,0:T(8,128)(2,1)}, u32[]{:S(2)}, u32[]{:S(2)}) collective-permute-start(bf16[1,16,1,32,128]{4,1,3,2,0:T(8,128)(2,1)} %add_convert_fusion), channel_id=1, source_target_pairs={{0,1},{1,2},{2,3},{3,4},{4,5},{5,6},{6,7},{7,8},{8,9},{9,10},{10,1... | collective-permute-start | bytes 393224 | tf_op jit(solution)/shard_map/ppermute | solution.py:14
  31.7 1.5 copy.41
  33.2 1.4 select_maximum_fusion.7
  35.0 0.9 constant_dynamic-update-slice_fusion.49
  36.7 0.9 constant_dynamic-update-slice_fusion.40
  38.4 0.9 constant_dynamic-update-slice_fusion.31
  39.7 0.9 copy.39
  40.7 1.2 fusion.22
  42.1 1.3 collective-permute-start.5
  43.4 4.2 %collective-permute-start.4 = (bf16[1,32,1,32,128]{4,1,3,2,0:T(8,128)(2,1)S(1)}, bf16[1,32,1,32,128]{4,1,3,2,0:T(8,128)(2,1)S(1)}, u32[]{:S(2)}, u32[]{:S(2)}) collective-permute-start(bf16[1,32,1,32,128]{4,1,3,2,0:T(8,128)(2,1)S(1)} %pad_maximum_fusion), channel_id=1, source_target_pairs={{0,1},{1,2},{2,3},{3,4},{4,5},{5,6},{6,7},{7,8},{8,9},{9,10},{10,1... | collective-permute-start | bytes 786440 | tf_op jit(solution)/shard_map/ppermute | solution.py:14
  47.6 1.2 fusion.37
  49.3 1.5 collective-permute-done.4
  50.7 2.3 select_maximum_fusion.3
  56.6 1.9 multiply_convert_fusion.1
  58.5 1.1 convolution_bitcast_fusion.1
  59.7 0.9 all_gather_reshape.3
  60.6 1.0 pad_maximum_fusion.1
  61.6 1.3 collective-permute-start.7
  62.9 5.0 %collective-permute-start.6 = (bf16[1,32,1,32,128]{4,1,3,2,0:T(8,128)(2,1)S(1)}, bf16[1,32,1,32,128]{4,1,3,2,0:T(8,128)(2,1)S(1)}, u32[]{:S(2)}, u32[]{:S(2)}) collective-permute-start(bf16[1,32,1,32,128]{4,1,3,2,0:T(8,128)(2,1)S(1)} %pad_maximum_fusion.1), channel_id=1, source_target_pairs={{0,1},{1,2},{2,3},{3,4},{4,5},{5,6},{6,7},{7,8},{8,9},{9,10},{10,1... | collective-permute-start | bytes 786440 | tf_op jit(solution)/shard_map/ppermute | solution.py:14
  67.9 0.9 copy.42
  69.5 1.5 collective-permute-done.6
  71.0 3.2 %select_maximum_fusion = bf16[1,32,3,34,130]{4,1,3,2,0:T(8,128)(2,1)S(1)} fusion(bf16[1,32,1,32,128]{4,1,3,2,0:T(8,128)(2,1)S(1)} %collective-permute-done.7, bf16[1,32,1,32,128]{4,1,3,2,0:T(8,128)(2,1)S(1)} %collective-permute-done.6, bf16[1,16,1,32,128]{4,1,3,2,0:T(8,128)(2,1)} %copy-done.2, bf16[1,16,1,32,128]{4,1,3,2,0:T(8,128)(2,1)} %copy-done), kind=kLoop, calls=%fused_computation.26 | loop fusion | flops 9759360 | bytes 1635072 | tf_op jit(solution)/shard_map/concatenate | solution.py:16
  75.0 0.9 fusion.68
  76.6 0.8 fusion.66
  78.9 0.8 fusion.64
  79.7 0.8 fusion.63
  81.3 0.8 fusion.61
  82.1 0.8 fusion.60
  83.7 0.8 fusion.58
  86.0 0.8 fusion.56
  86.9 0.8 fusion.55
  88.4 0.8 fusion.53
  89.3 0.8 fusion.52
  90.9 0.8 fusion.50
  93.2 0.8 fusion.48
  94.0 0.8 fusion.47
  95.6 127.1 %all-gather.2.cloned.1.call-done = f32[128,1,27648]{2,1,0:T(1,128)} async-done(((f32[1,1,27648]{2,1,0:T(1,128)}), f32[128,1,27648]{2,1,0:T(1,128)}) %all-gather.2.cloned.1.call-update) | async-done | bytes 14155792 | tf_op jit(solution)/shard_map/all_gather | solution.py:105
  222.8 10.7 %reduce_sum.16 = f32[27648]{0:T(1024)S(1)} reduce(f32[128,1,27648]{2,1,0:T(1,128)} %all-gather.2.cloned.1.call-done, f32[]{:T(128)} %constant.8.clone.1), dimensions={0,1}, to_apply=%region_0.1 | reduce | flops 3511296 | bytes 14266372 | tf_op jit(solution)/shard_map/reduce_sum | solution.py:106
  235.4 4.2 %fusion.31 = f32[1,16,1,32,128]{4,1,3,2,0:T(8,128)S(1)} fusion(f32[1,16,1,32,128]{4,1,3,2,0:T(8,128)S(1)} %copy-done.8, bf16[32,27,16,1]{0,2,3,1:T(8,128)(2,1)S(1)} %bitcast.513, bf16[1,27,32,1,32,128]{5,2,4,3,1,0:T(8,128)(2,1)} %fusion.46), kind=kOutput, calls=%fused_computation.43 | convolution fusion | flops 113311744 | bytes 7629824 | tf_op jit(solution)/shard_map/otc,etozhw->eczhw/dot_general | solution.py:59
  240.5 22.3 %all-reduce.6.cloned.1.call-done = f32[27648]{0:T(1024)} async-done(((f32[27648]{0:T(1024)}), f32[27648]{0:T(1024)}) %all-reduce.6.cloned.1.call-update) | async-done | bytes 110608 | tf_op jit(solution)/shard_map/psum | solution.py:110
  262.8 0.9 broadcast_multiply_fusion
  (139 shorter events, 25.3 us)
Async XLA Ops:
  7.2 11.1 %copy-start.6 = (bf16[1,16,1,32,128]{4,3,2,1,0:T(8,128)(2,1)S(1)}, bf16[1,16,1,32,128]{4,3,2,1,0:T(8,128)(2,1)}, u32[]{:S(2)}) copy-start(bf16[1,16,1,32,128]{4,3,2,1,0:T(8,128)(2,1)} %param.6) | copy-start | bytes 393220
  7.2 215.6 %all-gather.2.cloned.1.call-start = ((), (), s32[]{:S(2)}) async-start(), calls=%async_computation | async-start | bytes 14266368 | tf_op jit(solution)/shard_map/all_gather | solution.py:105
  7.2 8.1 %collective-permute-start.1 = (bf16[1,16,1,32,128]{4,3,2,1,0:T(8,128)(2,1)}, bf16[1,16,1,32,128]{4,3,2,1,0:T(8,128)(2,1)S(1)}, u32[]{:S(2)}, u32[]{:S(2)}) collective-permute-start(bf16[1,16,1,32,128]{4,3,2,1,0:T(8,128)(2,1)} %param.6), channel_id=1, source_target_pairs={{1,0},{2,1},{3,2},{4,3},{5,4},{6,5},{7,6},{8,7},{9,8},{10,9},{11,1... | collective-permute-start | bytes 393224 | tf_op jit(solution)/shard_map/ppermute | solution.py:15
  8.5 6.8 %collective-permute-start = (bf16[1,16,1,32,128]{4,3,1,2,0:T(8,128)(2,1)}, bf16[1,16,1,32,128]{4,3,1,2,0:T(8,128)(2,1)S(1)}, u32[]{:S(2)}, u32[]{:S(2)}) collective-permute-start(bf16[1,16,1,32,128]{4,3,1,2,0:T(8,128)(2,1)} %bitcast.509), channel_id=1, source_target_pairs={{0,1},{1,2},{2,3},{3,4},{4,5},{5,6},{6,7},{7,8},{8,9},{9,10},{10,1... | collective-permute-start | bytes 393224 | tf_op jit(solution)/shard_map/ppermute | solution.py:14
  19.8 1.4 copy-start.11
  21.2 1.6 copy-start.7
  22.0 0.8 copy-start.4
  23.5 9.7 %collective-permute-start.3 = (bf16[1,16,1,32,128]{4,1,3,2,0:T(8,128)(2,1)}, bf16[1,16,1,32,128]{4,1,3,2,0:T(8,128)(2,1)}, u32[]{:S(2)}, u32[]{:S(2)}) collective-permute-start(bf16[1,16,1,32,128]{4,1,3,2,0:T(8,128)(2,1)} %add_convert_fusion), channel_id=1, source_target_pairs={{1,0},{2,1},{3,2},{4,3},{5,4},{6,5},{7,6},{8,7},{9,8},{10,9},{11,1... | collective-permute-start | bytes 393224 | tf_op jit(solution)/shard_map/ppermute | solution.py:15
  24.8 8.4 %collective-permute-start.2 = (bf16[1,16,1,32,128]{4,1,3,2,0:T(8,128)(2,1)}, bf16[1,16,1,32,128]{4,1,3,2,0:T(8,128)(2,1)}, u32[]{:S(2)}, u32[]{:S(2)}) collective-permute-start(bf16[1,16,1,32,128]{4,1,3,2,0:T(8,128)(2,1)} %add_convert_fusion), channel_id=1, source_target_pairs={{0,1},{1,2},{2,3},{3,4},{4,5},{5,6},{6,7},{7,8},{8,9},{9,10},{10,1... | collective-permute-start | bytes 393224 | tf_op jit(solution)/shard_map/ppermute | solution.py:14
  39.7 1.0 copy-start.12
  40.7 1.2 copy-start.9
  40.7 1.2 copy-start.13
  42.1 7.1 %collective-permute-start.5 = (bf16[1,32,1,32,128]{4,1,3,2,0:T(8,128)(2,1)S(1)}, bf16[1,32,1,32,128]{4,1,3,2,0:T(8,128)(2,1)S(1)}, u32[]{:S(2)}, u32[]{:S(2)}) collective-permute-start(bf16[1,32,1,32,128]{4,1,3,2,0:T(8,128)(2,1)S(1)} %pad_maximum_fusion), channel_id=1, source_target_pairs={{1,0},{2,1},{3,2},{4,3},{5,4},{6,5},{7,6},{8,7},{9,8},{10,9},{11,1... | collective-permute-start | bytes 786440 | tf_op jit(solution)/shard_map/ppermute | solution.py:15
  43.4 7.3 %collective-permute-start.4 = (bf16[1,32,1,32,128]{4,1,3,2,0:T(8,128)(2,1)S(1)}, bf16[1,32,1,32,128]{4,1,3,2,0:T(8,128)(2,1)S(1)}, u32[]{:S(2)}, u32[]{:S(2)}) collective-permute-start(bf16[1,32,1,32,128]{4,1,3,2,0:T(8,128)(2,1)S(1)} %pad_maximum_fusion), channel_id=1, source_target_pairs={{0,1},{1,2},{2,3},{3,4},{4,5},{5,6},{6,7},{7,8},{8,9},{9,10},{10,1... | collective-permute-start | bytes 786440 | tf_op jit(solution)/shard_map/ppermute | solution.py:14
  54.9 1.7 copy-start.5
  54.9 1.7 copy-start.10
  58.5 1.1 copy-start
  58.5 1.1 copy-start.2
  60.6 202.2 %all-reduce.6.cloned.1.call-start = ((), (), s32[]{:S(2)}) async-start(), calls=%async_computation.1 | async-start | bytes 221184 | tf_op jit(solution)/shard_map/psum | solution.py:110
  61.6 7.9 %collective-permute-start.7 = (bf16[1,32,1,32,128]{4,1,3,2,0:T(8,128)(2,1)S(1)}, bf16[1,32,1,32,128]{4,1,3,2,0:T(8,128)(2,1)S(1)}, u32[]{:S(2)}, u32[]{:S(2)}) collective-permute-start(bf16[1,32,1,32,128]{4,1,3,2,0:T(8,128)(2,1)S(1)} %pad_maximum_fusion.1), channel_id=1, source_target_pairs={{1,0},{2,1},{3,2},{4,3},{5,4},{6,5},{7,6},{8,7},{9,8},{10,9},{11,1... | collective-permute-start | bytes 786440 | tf_op jit(solution)/shard_map/ppermute | solution.py:15
  62.9 8.0 %collective-permute-start.6 = (bf16[1,32,1,32,128]{4,1,3,2,0:T(8,128)(2,1)S(1)}, bf16[1,32,1,32,128]{4,1,3,2,0:T(8,128)(2,1)S(1)}, u32[]{:S(2)}, u32[]{:S(2)}) collective-permute-start(bf16[1,32,1,32,128]{4,1,3,2,0:T(8,128)(2,1)S(1)} %pad_maximum_fusion.1), channel_id=1, source_target_pairs={{0,1},{1,2},{2,3},{3,4},{4,5},{5,6},{6,7},{7,8},{8,9},{9,10},{10,1... | collective-permute-start | bytes 786440 | tf_op jit(solution)/shard_map/ppermute | solution.py:14
  74.1 10.5 %copy-start.1 = (bf16[1,16,1,32,128]{4,1,3,2,0:T(8,128)(2,1)S(1)}, bf16[1,16,1,32,128]{4,1,3,2,0:T(8,128)(2,1)}, u32[]{:S(2)}) copy-start(bf16[1,16,1,32,128]{4,1,3,2,0:T(8,128)(2,1)} %copy-done) | copy-start | bytes 393220
  74.1 10.4 %copy-start.3 = (bf16[1,16,1,32,128]{4,1,3,2,0:T(8,128)(2,1)S(1)}, bf16[1,16,1,32,128]{4,1,3,2,0:T(8,128)(2,1)}, u32[]{:S(2)}) copy-start(bf16[1,16,1,32,128]{4,1,3,2,0:T(8,128)(2,1)} %copy-done.2) | copy-start | bytes 393220
  95.6 139.8 %copy-start.8 = (f32[1,16,1,32,128]{4,1,3,2,0:T(8,128)S(1)}, f32[1,16,1,32,128]{4,1,3,2,0:T(8,128)}, u32[]{:S(2)}) copy-start(f32[1,16,1,32,128]{4,1,3,2,0:T(8,128)} %get-tuple-element.16) | copy-start | bytes 786436
Sparse Core Ops, SparseCore 0:
  60.7 162.0 all-gather.1
  235.6 27.1 all-reduce.5
